TPU v7x, 256 devices: a whole 4x4x8 slice. The times are simulated.
256 devices in a mesh: blk: 64 (over z, x, core), ch: 4 (over y).
Axes of the slice: x: 4, y: 4, z: 8, core: 2. Of those that a mesh axis runs over, the one named last changes fastest.
Arguments:
- features: bfloat16 [128, 65536], P('ch', 'blk'), may hold values from -6 to 6
- weight: bfloat16 [27, 128, 128], P(None, 'ch'), may hold values from -0.1875 to 0.1875
- grad_out: bfloat16 [128, 65536], P('ch', 'blk'), may hold values from -6 to 6
- rulebook: int32 [27, 65536], P(None, 'blk'), may hold values from 0 to 1280, as said below
Outputs:
- output: bfloat16 [128, 65536], P('ch', 'blk')
- grad_features: bfloat16 [128, 65536], P('ch', 'blk')
- weight_grad: float32 [27, 128, 128], P(None, 'ch')
Inputs may be any that keep to these rules, and one draw needn't show every extreme that they name: `rulebook`: slots 0 to 127 of every block hold active voxels of its lowest layer, slots 128 to 255 active voxels of its highest layer, then come active inner voxels, then empty slots; at least 640 slots of a block are active and some block has all 1024. Offset k = 9 (dx + 1) + 3 (dy + 1) + (dz + 1), dz along the block order. An entry names the table column of the active neighbour at that offset, and the zero column 1280 for an inactive neighbour, one outside the image, and for every entry of an empty slot. If entry k of slot i names slot j, entry 26 - k of j names i.
All inputs are finite; a program needn't handle non-finite values.
Results may differ from a plain program's by a relative error of at most 0.001.
Values may be sent and summed in bfloat16 or wider, within the bound.
No kernel may reach another device: no remote copies, remote signals or barrier semaphores. Data moves between devices by JAX's collectives and lax.ppermute only.
A program may use at most 64 MiB of HBM per device.

v0:
```python
import math
import jax
import jax.numpy as jnp
from jax import lax
from jax.sharding import PartitionSpec as P

VOX = 1024
FACE = 128


def passed_along(value, axis, steps):
    count = lax.axis_size(axis)
    pairs = [(source, (source + steps) % count) for source in range(count)]
    return lax.ppermute(value, axis, pairs)


def split_faces(source):
    chan_count = source.shape[0]
    blocks = source.reshape(chan_count, source.shape[1] // VOX, VOX)
    lowest = blocks[:, :, :FACE].reshape(chan_count, -1)
    highest = blocks[:, :, FACE : 2 * FACE].reshape(chan_count, -1)
    return (lowest, highest)


def align(from_lower, from_upper):
    chan_count = from_lower.shape[0]
    lower_faces = from_lower.reshape(chan_count, -1, FACE)
    upper_faces = from_upper.reshape(chan_count, -1, FACE)
    blank_faces = jnp.zeros_like(lower_faces)
    position = lax.axis_index("blk")
    final_index = lax.axis_size("blk") - 1
    lower_faces = jnp.where(
        position == 0, jnp.concatenate([blank_faces, lower_faces[:, :-1]], axis=1), lower_faces
    )
    upper_faces = jnp.where(
        position == final_index,
        jnp.concatenate([upper_faces[:, 1:], blank_faces], axis=1),
        upper_faces,
    )
    return (lower_faces.reshape(chan_count, -1), upper_faces.reshape(chan_count, -1))


def extend(source, lower_faces, upper_faces):
    zero_column = jnp.zeros((source.shape[0], 1), source.dtype)
    return jnp.concatenate([source, lower_faces, upper_faces, zero_column], axis=1)


def densify(table, neighbours):
    table_rows = table.T
    picked_rows = jnp.take(table_rows, neighbours, axis=0)
    return picked_rows.reshape(neighbours.shape[0], -1)


def per_device(features, weight, grad_out, rulebook):
    quarter = features.shape[0]
    local_rows = features.shape[1]
    width = weight.shape[2]
    neighbours = rulebook.T
    lowest, highest = split_faces(features)
    from_lower = passed_along(highest, "blk", 1)
    from_upper = passed_along(lowest, "blk", -1)
    lower_faces, upper_faces = align(from_lower, from_upper)
    ext_inputs = extend(features, lower_faces, upper_faces)
    dense_inputs = densify(ext_inputs, neighbours)
    flat_weight = weight.reshape(27 * quarter, width)
    output = lax.psum_scatter(
        jnp.dot(dense_inputs, flat_weight, preferred_element_type=jnp.float32).T,
        "ch",
        scatter_dimension=0,
        tiled=True,
    )
    output = output.astype(jnp.bfloat16)
    grad_full = lax.all_gather(grad_out, "ch", axis=0, tiled=True)
    grad_lowest, grad_highest = split_faces(grad_full)
    grad_lower = passed_along(grad_highest, "blk", 1)
    grad_upper = passed_along(grad_lowest, "blk", -1)
    lower_grads, upper_grads = align(grad_lower, grad_upper)
    ext_grads = extend(grad_full, lower_grads, upper_grads)
    flipped = neighbours[:, ::-1]
    dense_grads = densify(ext_grads, flipped)
    back_weight = weight.transpose(0, 2, 1).reshape(27 * width, quarter)
    grad_inputs = jnp.dot(dense_grads, back_weight, preferred_element_type=jnp.float32).T
    local_terms = lax.dot_general(
        dense_inputs, grad_full.T, (((0,), (0,)), ((), ())), preferred_element_type=jnp.float32
    )
    local_terms = local_terms.reshape(27, quarter, width)
    norm_scale = 1.0 / math.sqrt(lax.axis_size("blk") * local_rows)
    weight_grad = lax.psum(local_terms, "blk") * norm_scale
    return (output, grad_inputs.astype(jnp.bfloat16), weight_grad)


def solution(mesh):
    placed = (P("ch", "blk"), P(None, "ch", None), P("ch", "blk"), P(None, "blk"))
    return jax.shard_map(
        per_device,
        mesh=mesh,
        in_specs=placed,
        out_specs=(P("ch", "blk"), P("ch", "blk"), P(None, "ch", None)),
        check_vma=False,
    )
```

profile of v0, /device:TPU:1, one launch (start us, length us, event | category | flops | bytes accessed | tf_op | source)
XLA Modules:
  0.0 368.4 jit_solution(6934085552225605736)
XLA Ops:
  8.0 0.0 copy-start
  8.0 0.0 all-reduce.2.cloned.1.call-start
  8.1 11.6 %all_gather.3 = bf16[128,1024]{1,0:T(8,128)(2,1)S(1)} all-gather(bf16[32,1024]{1,0:T(8,128)(2,1)} %param.6), channel_id=1, replica_groups=mesh['blk'=64,'ch'=4] {'ch'}, dimensions={0}, use_global_device_ids=true | all-gather | bytes 327680 | tf_op jit(solution)/shard_map/all_gather | solution.py:73
  19.7 4.7 %collective-permute-start.3 = (bf16[128,128]{1,0:T(8,128)(2,1)S(1)}, bf16[128,128]{1,0:T(8,128)(2,1)S(1)}, u32[]{:S(2)}, u32[]{:S(2)}) collective-permute-start(bf16[128,128]{1,0:T(8,128)(2,1)S(1)} %get-tuple-element.16), channel_id=1, source_target_pairs={{0,252},{4,0},{8,4},{12,8},{16,12},{20,16},{24,20},{28,24},{32,28}... | collective-permute-start | bytes 98312 | tf_op jit(solution)/shard_map/ppermute | solution.py:14
  24.3 0.0 collective-permute-start.2
  24.3 0.7 slice_bitcast_fusion.3
  25.0 3.6 collective-permute-start.1
  28.6 0.0 collective-permute-start
  28.6 2.9 rev.3
  31.6 0.9 compare_select_fusion.1
  32.6 0.2 copy.44
  32.8 0.4 reshape.76
  33.2 0.2 copy.39
  33.4 0.4 reshape.68
  33.8 0.9 compare_and_fusion.1
  34.7 0.3 copy.43
  35.0 0.3 copy.37
  35.3 0.0 collective-permute-done.1
  35.3 0.0 collective-permute-done
  35.4 0.9 maximum_maximum_fusion
  36.2 0.2 copy.38
  36.5 96.4 %gather_fusion = bf16[27648,32]{1,0:T(8,128)(2,1)} fusion(bf16[1281,32]{1,0:T(8,128)(2,1)S(1)} %bitcast.48, s32[27648]{0:T(1024)S(1)} %broadcast_clamp_fusion.1), kind=kCustom, calls=%fused_computation | custom fusion | bytes 3649536 | tf_op jit(solution)/shard_map/jit(_take)/gather | solution.py:50
  132.9 5.4 %copy.40 = bf16[27648,32]{0,1:T(8,128)(2,1)S(1)} copy(bf16[27648,32]{1,0:T(8,128)(2,1)} %gather_fusion) | data formatting | bytes 3538944 | tf_op jit(solution)/shard_map/jit(_take)/gather | solution.py:50
  138.3 22.7 %reshape.67 = bf16[1024,27,32]{1,0,2:T(8,128)(2,1)} reshape(bf16[27648,32]{0,1:T(8,128)(2,1)S(1)} %copy.40) | data formatting | bytes 3538944 | tf_op jit(solution)/shard_map/jit(_take)/gather | solution.py:50
  161.0 7.7 %broadcast_select_fusion.1 = bf16[1024,27,32]{1,0,2:T(8,128)(2,1)} fusion(bf16[1024,27,32]{1,0,2:T(8,128)(2,1)} %reshape.67, pred[1024,27]{1,0:T(8,128)(4,1)S(1)} %copy.37), kind=kLoop, calls=%fused_computation.3 | loop fusion | flops 884736 | bytes 3566592 | tf_op jit(solution)/shard_map/jit(_take)/select_n | solution.py:50
  168.7 7.5 %copy.47 = bf16[1024,27,32]{0,2,1:T(8,128)(2,1)S(1)} copy(bf16[1024,27,32]{1,0,2:T(8,128)(2,1)} %broadcast_select_fusion.1) | data formatting | bytes 3538944 | tf_op jit(solution)/shard_map/jit(_take)/select_n | solution.py:50
  176.3 1.4 fusion.2
  177.7 0.0 all-reduce.2.cloned.1.call-update
  177.7 0.2 reduce-scatter.4.cloned.1.call-start
  177.9 0.0 copy-done
  177.9 5.1 %convolution_bitcast_fusion = f32[128,1024]{0,1:T(8,128)S(1)} fusion(bf16[1024,27,32]{1,0,2:T(8,128)(2,1)} %broadcast_select_fusion.1, bf16[27,32,128]{2,1,0:T(8,128)(2,1)S(1)} %copy-done), kind=kOutput, calls=%fused_computation.8 | convolution fusion | flops 226492416 | bytes 2514944 | tf_op jit(solution)/shard_map/dot_general | solution.py:67
  183.1 1.0 copy.50
  184.1 0.0 reduce-scatter.4.cloned.1.call-update
  184.1 0.0 collective-permute-done.3
  184.1 0.0 collective-permute-done.2
  184.2 0.1 maximum_bitcast_fusion
  184.2 0.2 copy.45
  184.4 96.4 %gather_fusion.1 = bf16[27648,128]{1,0:T(8,128)(2,1)} fusion(bf16[1281,128]{1,0:T(8,128)(2,1)S(1)} %copy.45, s32[27648]{0:T(1024)S(1)} %broadcast_clamp_fusion), kind=kCustom, calls=%fused_computation.1 | custom fusion | bytes 14266368 | tf_op jit(solution)/shard_map/jit(_take)/gather | solution.py:50
  280.8 11.9 %reshape.75 = bf16[1024,27,128]{2,1,0:T(8,128)(2,1)} reshape(bf16[27648,128]{1,0:T(8,128)(2,1)} %gather_fusion.1) | data formatting | bytes 14155776 | tf_op jit(solution)/shard_map/jit(_take)/gather | solution.py:50
  292.7 15.3 %broadcast_select_fusion = bf16[1024,27,128]{2,1,0:T(8,128)(2,1)S(1)} fusion(bf16[1024,27,128]{2,1,0:T(8,128)(2,1)} %reshape.75, pred[1024,27]{1,0:T(8,128)(4,1)S(1)} %copy.43), kind=kLoop, calls=%fused_computation.2 | loop fusion | flops 3538944 | bytes 14183424 | tf_op jit(solution)/shard_map/jit(_take)/select_n | solution.py:50
  308.1 4.3 %fusion.10 = bf16[32,1024]{1,0:T(8,128)(2,1)} fusion(bf16[1024,27,128]{2,1,0:T(8,128)(2,1)S(1)} %broadcast_select_fusion, bf16[27,32,128]{2,1,0:T(8,128)(2,1)S(1)} %copy-done), kind=kOutput, calls=%fused_computation.11 | convolution fusion | flops 226525184 | bytes 7364608 | tf_op jit(solution)/shard_map/dot_general | solution.py:82
  312.4 44.9 %all-reduce.2.cloned.1.call-done = f32[27,32,128]{2,1,0:T(8,128)} async-done(((f32[27,32,128]{2,1,0:T(8,128)}), f32[27,32,128]{2,1,0:T(8,128)}) %all-reduce.2.cloned.1.call-update) | async-done | bytes 442384 | tf_op jit(solution)/shard_map/psum | solution.py:88
  357.3 1.8 broadcast_multiply_fusion
  359.1 0.0 reduce-scatter.4.cloned.1.call-done
  359.1 1.1 copy.51
  360.2 0.8 copy.48
  (10 shorter events, 0.2 us)
Async XLA Ops:
  8.0 169.9 %copy-start = (bf16[27,32,128]{2,1,0:T(8,128)(2,1)S(1)}, bf16[27,32,128]{2,1,0:T(8,128)(2,1)}, u32[]{:S(2)}) copy-start(bf16[27,32,128]{2,1,0:T(8,128)(2,1)} %param.5) | copy-start | bytes 663556
  8.0 349.3 %all-reduce.2.cloned.1.call-start = ((), (), s32[]{:S(2)}) async-start(), calls=%async_computation.1 | async-start | bytes 884736 | tf_op jit(solution)/shard_map/psum | solution.py:88
  19.7 164.4 %collective-permute-start.3 = (bf16[128,128]{1,0:T(8,128)(2,1)S(1)}, bf16[128,128]{1,0:T(8,128)(2,1)S(1)}, u32[]{:S(2)}, u32[]{:S(2)}) collective-permute-start(bf16[128,128]{1,0:T(8,128)(2,1)S(1)} %get-tuple-element.16), channel_id=1, source_target_pairs={{0,252},{4,0},{8,4},{12,8},{16,12},{20,16},{24,20},{28,24},{32,28}... | collective-permute-start | bytes 98312 | tf_op jit(solution)/shard_map/ppermute | solution.py:14
  24.3 159.8 %collective-permute-start.2 = (bf16[128,128]{1,0:T(8,128)(2,1)S(1)}, bf16[128,128]{1,0:T(8,128)(2,1)S(1)}, u32[]{:S(2)}, u32[]{:S(2)}) collective-permute-start(bf16[128,128]{1,0:T(8,128)(2,1)S(1)} %get-tuple-element.15), channel_id=1, source_target_pairs={{0,4},{4,8},{8,12},{12,16},{16,20},{20,24},{24,28},{28,32},{32,36}... | collective-permute-start | bytes 98312 | tf_op jit(solution)/shard_map/ppermute | solution.py:14
  25.0 10.3 %collective-permute-start.1 = (bf16[32,128]{1,0:T(8,128)(2,1)S(1)}, bf16[32,128]{1,0:T(8,128)(2,1)S(1)}, u32[]{:S(2)}, u32[]{:S(2)}) collective-permute-start(bf16[32,128]{1,0:T(8,128)(2,1)S(1)} %get-tuple-element.18), channel_id=1, source_target_pairs={{0,252},{4,0},{8,4},{12,8},{16,12},{20,16},{24,20},{28,24},{32,28}... | collective-permute-start | bytes 24584 | tf_op jit(solution)/shard_map/ppermute | solution.py:14
  28.6 6.7 %collective-permute-start = (bf16[32,128]{1,0:T(8,128)(2,1)S(1)}, bf16[32,128]{1,0:T(8,128)(2,1)S(1)}, u32[]{:S(2)}, u32[]{:S(2)}) collective-permute-start(bf16[32,128]{1,0:T(8,128)(2,1)S(1)} %get-tuple-element.17), channel_id=1, source_target_pairs={{0,4},{4,8},{8,12},{12,16},{16,20},{20,24},{24,28},{28,32},{32,36}... | collective-permute-start | bytes 24584 | tf_op jit(solution)/shard_map/ppermute | solution.py:14
  177.7 181.4 %reduce-scatter.4.cloned.1.call-start = ((), (), s32[]{:S(2)}) async-start(), calls=%async_computation.2 | async-start | bytes 655360
Sparse Core Ops, SparseCore 0:
  177.8 179.4 all-reduce.1
Sparse Core Ops, SparseCore 1:
  184.2 23.4 reduce-scatter.3
where the time goes:
time: 370 us; the launch traced here: 368 us
  local copies, waits for them, and re-layouts  249 us (67%)
  waiting for transfers between devices  44.9 us (12%)
  other arithmetic  27.8 us (8%)
  between operations  15.7 us (4%)
  blocking collectives  11.6 us (3%)
  matrix products  10.9 us (3%)
  starting transfers between devices  8.51 us (2%)
    gather x5, local copies, waits for them, and re-layouts, densify(): picked_rows = jnp.take(table_rows, neighbours, axis=0)  233 us
    psum x1, waiting for transfers between devices, per_device(): weight_grad = lax.psum(local_terms, 'blk') * norm_scale  44.9 us
    select_n x4, other arithmetic, densify(): picked_rows = jnp.take(table_rows, neighbours, axis=0)  24 us
    all_gather x1, blocking collectives, per_device(): grad_full = lax.all_gather(grad_out, 'ch', axis=0, tiled=True)  11.6 us
    ppermute x4, starting transfers between devices, passed_along(): return lax.ppermute(value, axis, pairs)  8.25 us
    select_n x3, local copies, waits for them, and re-layouts, densify(): picked_rows = jnp.take(table_rows, neighbours, axis=0)  7.95 us
  transfers between devices with their start and end apart: 6, of which 1 were waited for; matrix products, arithmetic and copies ran while one was open for 78% of the time, Pallas kernels for 0%

commit v1 on v0

--- a/solution.py
+++ b/solution.py
@@ -6,6 +6,11 @@
 
 VOX = 1024
 FACE = 128
+
+
+def summed_here(value, axis):
+    parts = lax.all_gather(value, axis)
+    return jnp.sum(parts, axis=0)
 
 
 def passed_along(value, axis, steps):
@@ -85,7 +90,7 @@
     )
     local_terms = local_terms.reshape(27, quarter, width)
     norm_scale = 1.0 / math.sqrt(lax.axis_size("blk") * local_rows)
-    weight_grad = lax.psum(local_terms, "blk") * norm_scale
+    weight_grad = summed_here(local_terms, "blk") * norm_scale
     return (output, grad_inputs.astype(jnp.bfloat16), weight_grad)
 
 

time: 370 us -> 341 us (0.922)
  waiting for transfers between devices: 44.9 us -> 3.65 us
  other arithmetic: 27.8 us -> 37.2 us
  starting transfers between devices: 8.51 us -> 12.5 us
    psum x1 -> x0, waiting for transfers between devices: 44.9 us -> none  [per_device(): weight_grad = lax.psum(local_terms, 'blk') * norm_scale]
    reduce_sum x0 -> x1, other arithmetic: none -> 10.4 us  [summed_here(): return jnp.sum(parts, axis=0)]
    ppermute x4, starting transfers between devices: 8.25 us -> 12.4 us  [passed_along(): return lax.ppermute(value, axis, pairs)]
  transfers between devices with their start and end apart: 6 -> 6, of which waited for: 1 -> 1; matrix products, arithmetic and copies ran while one was open for 78% -> 43% of each run, Pallas kernels for 0% -> 0%
where the time goes in v1:
time: 341 us; the launch traced here: 336 us
  local copies, waits for them, and re-layouts  246 us (72%)
  other arithmetic  37.2 us (11%)
  between operations  15.7 us (5%)
  starting transfers between devices  12.5 us (4%)
  matrix products  10.9 us (3%)
  blocking collectives  9.89 us (3%)
  waiting for transfers between devices  3.65 us (1%)
    gather x5, local copies, waits for them, and re-layouts, densify(): picked_rows = jnp.take(table_rows, neighbours, axis=0)  233 us
    select_n x4, other arithmetic, densify(): picked_rows = jnp.take(table_rows, neighbours, axis=0)  24 us
    ppermute x4, starting transfers between devices, passed_along(): return lax.ppermute(value, axis, pairs)  12.4 us
    reduce_sum x1, other arithmetic, summed_here(): return jnp.sum(parts, axis=0)  10.4 us
    all_gather x1, blocking collectives, per_device(): grad_full = lax.all_gather(grad_out, 'ch', axis=0, tiled=True)  9.89 us
    select_n x3, local copies, waits for them, and re-layouts, densify(): picked_rows = jnp.take(table_rows, neighbours, axis=0)  7.96 us
  transfers between devices with their start and end apart: 6, of which 1 were waited for; matrix products, arithmetic and copies ran while one was open for 43% of the time, Pallas kernels for 0%

profile of v1, /device:TPU:1, one launch (start us, length us, event | category | flops | bytes accessed | tf_op | source)
XLA Modules:
  0.0 336.2 jit_solution(4780977653362426986)
XLA Ops:
  8.0 0.0 copy-start
  8.0 0.0 reduce-scatter.4.cloned.1.call-start
  8.1 0.8 slice_bitcast_fusion.3
  8.8 3.2 collective-permute-start.1
  12.1 0.0 collective-permute-start
  12.1 0.9 compare_select_fusion.1
  13.0 0.2 copy.39
  13.2 0.4 reshape.73
  13.6 0.9 compare_and_fusion.1
  14.6 0.3 copy.37
  14.9 0.0 collective-permute-done.1
  14.9 3.6 %collective-permute-done = bf16[32,128]{1,0:T(8,128)(2,1)S(1)} collective-permute-done((bf16[32,128]{1,0:T(8,128)(2,1)S(1)}, bf16[32,128]{1,0:T(8,128)(2,1)S(1)}, u32[]{:S(2)}, u32[]{:S(2)}) %collective-permute-start) | collective-permute-done | bytes 8224 | tf_op jit(solution)/shard_map/ppermute | solution.py:19
  18.5 0.9 maximum_maximum_fusion
  19.4 0.2 copy.38
  19.6 96.4 %gather_fusion = bf16[27648,32]{1,0:T(8,128)(2,1)} fusion(bf16[1281,32]{1,0:T(8,128)(2,1)S(1)} %bitcast.49, s32[27648]{0:T(1024)S(1)} %broadcast_clamp_fusion.1), kind=kCustom, calls=%fused_computation | custom fusion | bytes 3649536 | tf_op jit(solution)/shard_map/jit(_take)/gather | solution.py:55
  116.0 5.4 %copy.40 = bf16[27648,32]{0,1:T(8,128)(2,1)S(1)} copy(bf16[27648,32]{1,0:T(8,128)(2,1)} %gather_fusion) | data formatting | bytes 3538944 | tf_op jit(solution)/shard_map/jit(_take)/gather | solution.py:55
  121.4 22.7 %reshape.72 = bf16[1024,27,32]{1,0,2:T(8,128)(2,1)} reshape(bf16[27648,32]{0,1:T(8,128)(2,1)S(1)} %copy.40) | data formatting | bytes 3538944 | tf_op jit(solution)/shard_map/jit(_take)/gather | solution.py:55
  144.1 7.7 %broadcast_select_fusion.1 = bf16[1024,27,32]{1,0,2:T(8,128)(2,1)} fusion(bf16[1024,27,32]{1,0,2:T(8,128)(2,1)} %reshape.72, pred[1024,27]{1,0:T(8,128)(4,1)S(1)} %copy.37), kind=kLoop, calls=%fused_computation.3 | loop fusion | flops 884736 | bytes 3566592 | tf_op jit(solution)/shard_map/jit(_take)/select_n | solution.py:55
  151.8 0.0 copy-done
  151.8 0.0 copy-start.2
  151.8 5.2 %convolution_bitcast_fusion = f32[128,1024]{0,1:T(8,128)S(1)} fusion(bf16[1024,27,32]{1,0,2:T(8,128)(2,1)} %broadcast_select_fusion.1, bf16[27,32,128]{2,1,0:T(8,128)(2,1)S(1)} %copy-done), kind=kOutput, calls=%fused_computation.8 | convolution fusion | flops 226492416 | bytes 2514944 | tf_op jit(solution)/shard_map/dot_general | solution.py:72
  157.0 0.0 copy-start.1
  157.0 1.0 copy.50
  158.0 0.0 reduce-scatter.4.cloned.1.call-update
  158.0 0.0 all-gather.3.cloned.1.call-start
  158.0 0.0 copy-done.2
  158.1 9.9 %all_gather.6 = bf16[128,1024]{1,0:T(8,128)(2,1)S(1)} all-gather(bf16[32,1024]{1,0:T(8,128)(2,1)S(1)} %copy-done.2), channel_id=1, replica_groups=mesh['blk'=64,'ch'=4] {'ch'}, dimensions={0}, use_global_device_ids=true | all-gather | bytes 327680 | tf_op jit(solution)/shard_map/all_gather | solution.py:78
  167.9 7.5 %copy.47 = bf16[1024,27,32]{0,2,1:T(8,128)(2,1)S(1)} copy(bf16[1024,27,32]{1,0,2:T(8,128)(2,1)} %broadcast_select_fusion.1) | data formatting | bytes 3538944 | tf_op jit(solution)/shard_map/jit(_take)/select_n | solution.py:55
  175.5 1.4 fusion.2
  176.9 0.0 all-gather.3.cloned.1.call-update
  176.9 9.2 %collective-permute-start.3 = (bf16[128,128]{1,0:T(8,128)(2,1)S(1)}, bf16[128,128]{1,0:T(8,128)(2,1)S(1)}, u32[]{:S(2)}, u32[]{:S(2)}) collective-permute-start(bf16[128,128]{1,0:T(8,128)(2,1)S(1)} %get-tuple-element.16), channel_id=1, source_target_pairs={{0,252},{4,0},{8,4},{12,8},{16,12},{20,16},{24,20},{28,24},{32,28}... | collective-permute-start | bytes 98312 | tf_op jit(solution)/shard_map/ppermute | solution.py:19
  186.1 0.0 collective-permute-start.2
  186.1 0.0 copy-done.1
  186.1 0.2 rev.3
  186.3 0.2 copy.44
  186.6 0.4 reshape.81
  187.0 0.3 copy.43
  187.3 0.0 collective-permute-done.3
  187.3 0.0 collective-permute-done.2
  187.3 0.1 maximum_bitcast_fusion
  187.4 0.2 copy.45
  187.6 96.4 %gather_fusion.1 = bf16[27648,128]{1,0:T(8,128)(2,1)} fusion(bf16[1281,128]{1,0:T(8,128)(2,1)S(1)} %copy.45, s32[27648]{0:T(1024)S(1)} %broadcast_clamp_fusion), kind=kCustom, calls=%fused_computation.1 | custom fusion | bytes 14266368 | tf_op jit(solution)/shard_map/jit(_take)/gather | solution.py:55
  284.0 12.0 %reshape.80 = bf16[1024,27,128]{2,1,0:T(8,128)(2,1)} reshape(bf16[27648,128]{1,0:T(8,128)(2,1)} %gather_fusion.1) | data formatting | bytes 14155776 | tf_op jit(solution)/shard_map/jit(_take)/gather | solution.py:55
  296.1 15.4 %broadcast_select_fusion = bf16[1024,27,128]{2,1,0:T(8,128)(2,1)S(1)} fusion(bf16[1024,27,128]{2,1,0:T(8,128)(2,1)} %reshape.80, pred[1024,27]{1,0:T(8,128)(4,1)S(1)} %copy.43), kind=kLoop, calls=%fused_computation.2 | loop fusion | flops 3538944 | bytes 14183424 | tf_op jit(solution)/shard_map/jit(_take)/select_n | solution.py:55
  311.4 4.3 %fusion.10 = bf16[32,1024]{1,0:T(8,128)(2,1)} fusion(bf16[1024,27,128]{2,1,0:T(8,128)(2,1)S(1)} %broadcast_select_fusion, bf16[27,32,128]{2,1,0:T(8,128)(2,1)S(1)} %copy-done), kind=kOutput, calls=%fused_computation.11 | convolution fusion | flops 226525184 | bytes 7364608 | tf_op jit(solution)/shard_map/dot_general | solution.py:87
  315.7 0.0 reduce-scatter.4.cloned.1.call-done
  315.7 1.1 copy.51
  316.8 0.8 copy.48
  317.6 0.0 all-gather.3.cloned.1.call-done
  317.6 10.4 %reduce_sum.9 = f32[27,32,128]{2,1,0:T(8,128)S(1)} reduce(f32[64,27,32,128]{3,2,1,0:T(8,128)} %bitcast.50, f32[]{:T(128)} %constant.44.clone.1), dimensions={0}, to_apply=%region_1.2 | reduce | flops 6967296 | bytes 28753924 | tf_op jit(solution)/shard_map/reduce_sum | solution.py:13
  328.0 0.8 broadcast_multiply_fusion
  (10 shorter events, 0.2 us)
Async XLA Ops:
  8.0 143.8 %copy-start = (bf16[27,32,128]{2,1,0:T(8,128)(2,1)S(1)}, bf16[27,32,128]{2,1,0:T(8,128)(2,1)}, u32[]{:S(2)}) copy-start(bf16[27,32,128]{2,1,0:T(8,128)(2,1)} %param.5) | copy-start | bytes 663556
  8.0 307.7 %reduce-scatter.4.cloned.1.call-start = ((), (), s32[]{:S(2)}) async-start(), calls=%async_computation.2 | async-start | bytes 655360
  8.8 6.0 %collective-permute-start.1 = (bf16[32,128]{1,0:T(8,128)(2,1)S(1)}, bf16[32,128]{1,0:T(8,128)(2,1)S(1)}, u32[]{:S(2)}, u32[]{:S(2)}) collective-permute-start(bf16[32,128]{1,0:T(8,128)(2,1)S(1)} %get-tuple-element.18), channel_id=1, source_target_pairs={{0,252},{4,0},{8,4},{12,8},{16,12},{20,16},{24,20},{28,24},{32,28}... | collective-permute-start | bytes 24584 | tf_op jit(solution)/shard_map/ppermute | solution.py:19
  12.1 6.4 %collective-permute-start = (bf16[32,128]{1,0:T(8,128)(2,1)S(1)}, bf16[32,128]{1,0:T(8,128)(2,1)S(1)}, u32[]{:S(2)}, u32[]{:S(2)}) collective-permute-start(bf16[32,128]{1,0:T(8,128)(2,1)S(1)} %get-tuple-element.17), channel_id=1, source_target_pairs={{0,4},{4,8},{8,12},{12,16},{16,20},{20,24},{24,28},{28,32},{32,36}... | collective-permute-start | bytes 24584 | tf_op jit(solution)/shard_map/ppermute | solution.py:19
  151.8 6.3 %copy-start.2 = (bf16[32,1024]{1,0:T(8,128)(2,1)S(1)}, bf16[32,1024]{1,0:T(8,128)(2,1)}, u32[]{:S(2)}) copy-start(bf16[32,1024]{1,0:T(8,128)(2,1)} %param.6) | copy-start | bytes 196612
  157.0 29.1 %copy-start.1 = (s32[27,1024]{1,0:T(8,128)S(1)}, s32[27,1024]{1,0:T(8,128)}, u32[]{:S(2)}) copy-start(s32[27,1024]{1,0:T(8,128)} %param.7) | copy-start | bytes 331780
  158.0 159.6 %all-gather.3.cloned.1.call-start = ((), (), s32[]{:S(2)}) async-start(), calls=%async_computation.1 | async-start | bytes 28753920 | tf_op jit(solution)/shard_map/all_gather | solution.py:12
  176.9 10.4 %collective-permute-start.3 = (bf16[128,128]{1,0:T(8,128)(2,1)S(1)}, bf16[128,128]{1,0:T(8,128)(2,1)S(1)}, u32[]{:S(2)}, u32[]{:S(2)}) collective-permute-start(bf16[128,128]{1,0:T(8,128)(2,1)S(1)} %get-tuple-element.16), channel_id=1, source_target_pairs={{0,252},{4,0},{8,4},{12,8},{16,12},{20,16},{24,20},{28,24},{32,28}... | collective-permute-start | bytes 98312 | tf_op jit(solution)/shard_map/ppermute | solution.py:19
  186.1 1.2 collective-permute-start.2
Sparse Core Ops, SparseCore 0:
  158.1 23.3 reduce-scatter.3
Sparse Core Ops, SparseCore 1:
  177.0 131.7 all-gather.2
